TPU v7x, 128 devices: a whole 4x4x4 slice. The times are simulated.
128 devices in a mesh: tm: 16 (over x, y_lo, core), space: 8 (over z, y_hi).
Axes of the slice: x: 4, y: 4 (y_hi: 2, y_lo: 2; y = y_hi * 2 + y_lo), z: 4, core: 2. Of those that a mesh axis runs over, the one named last changes fastest.
Arguments:
- input_field: float32 [64, 32, 32, 1024], P('tm', None, 'space'), may hold values from -6 to 6
- cotangent: float32 [64, 32, 32, 1024], P('tm', None, 'space'), may hold values from -6 to 6
- spectral_weights: float32 [2, 2, 16, 32, 32], replicated, may hold values from -0.75 to 0.75
- conv_kernel: float32 [2, 3, 32, 32], replicated, may hold values from -0.625 to 0.625
- mode_list: int32 [16], replicated, may hold values from 0 to 31, as said below
Outputs:
- grad_input: float32 [64, 32, 32, 1024], P('tm', None, 'space')
- grad_spectral: float32 [2, 2, 16, 32, 32], P(None, None, 'tm')
- grad_kernel: float32 [2, 3, 32, 32], replicated
Inputs may be any that keep to these rules, and one draw needn't show every extreme that they name: `mode_list`: 16 distinct frequencies in ascending order, with 0 and 31 among them.
All inputs are finite; a program needn't handle non-finite values.
Results may differ from a plain program's by a relative error of at most 0.00014.
Values sent between devices are 32-bit elements; how exact they have to be, the bound alone decides.
No kernel may reach another device: no remote copies, remote signals or barrier semaphores. Data moves between devices by JAX's collectives and lax.ppermute only.
A program may use at most 128 MiB of HBM per device.

v0:
```python
import math

import jax
import jax.numpy as jnp
from jax import lax
from jax.sharding import PartitionSpec as P

HIGHEST = lax.Precision.HIGHEST


def extended(value, sides, width):
    for axis, dim in sides:
        size, length = (lax.axis_size(axis), value.shape[dim])
        up = [(i, (i + 1) % size) for i in range(size - 1)]
        down = [(j, i) for i, j in up]
        last = lax.slice_in_dim(value, length - width, length, axis=dim)
        initial = lax.slice_in_dim(value, 0, width, axis=dim)
        before = lax.ppermute(last, axis, up)
        after = lax.ppermute(initial, axis, down)
        value = jnp.concatenate([before, value, after], axis=dim)
    return value


def tables(mode_list, time_count, total_time):
    time_steps = jnp.arange(time_count, dtype=jnp.int32)
    phase_index = mode_list[:, None] * time_steps[None, :] % total_time
    angles = phase_index.astype(jnp.float32) * (2.0 * math.pi / total_time)
    return (jnp.cos(angles), jnp.sin(angles))


def forward_dft(cosine_table, sine_table, flattened):
    time_count = flattened.shape[0]
    rows = flattened.reshape(time_count, -1)
    cosine_part = jnp.dot(cosine_table, rows, precision=HIGHEST)
    sine_part = -jnp.dot(sine_table, rows, precision=HIGHEST)
    stacked = jnp.stack([cosine_part, sine_part], axis=1)
    return stacked.reshape(cosine_table.shape[0], 2, flattened.shape[1], flattened.shape[2])


def inverse_dft(cosine_table, sine_table, coefficients, factor):
    mode_count = coefficients.shape[0]
    cosine_term = jnp.dot(
        cosine_table.T, coefficients[:, 0].reshape(mode_count, -1), precision=HIGHEST
    )
    sine_term = jnp.dot(sine_table.T, coefficients[:, 1].reshape(mode_count, -1), precision=HIGHEST)
    result = factor * (cosine_term - sine_term)
    return result.reshape(cosine_table.shape[1], coefficients.shape[2], coefficients.shape[3])


def mode_product(values, weight):
    return jnp.einsum("mcn,mcd->mdn", values, weight, precision=HIGHEST)


def mode_adjoint(values, weight):
    return jnp.einsum("mdn,mcd->mcn", values, weight, precision=HIGHEST)


def mode_outer(left_values, right_values):
    return jnp.einsum("mcn,mdn->mcd", left_values, right_values, precision=HIGHEST)


def channel_mix(coefficients, weight):
    real_part = mode_product(coefficients[:, 0], weight[0]) - mode_product(
        coefficients[:, 1], weight[1]
    )
    imag_part = mode_product(coefficients[:, 1], weight[0]) + mode_product(
        coefficients[:, 0], weight[1]
    )
    return jnp.stack([real_part, imag_part], axis=1)


def channel_mix_adjoint(sens_modes, weight):
    real_part = mode_adjoint(sens_modes[:, 0], weight[0]) + mode_adjoint(
        sens_modes[:, 1], weight[1]
    )
    imag_part = mode_adjoint(sens_modes[:, 1], weight[0]) - mode_adjoint(
        sens_modes[:, 0], weight[1]
    )
    return jnp.stack([real_part, imag_part], axis=1)


def weight_grad(coefficients, sens_modes):
    real_part = mode_outer(coefficients[:, 0], sens_modes[:, 0]) + mode_outer(
        coefficients[:, 1], sens_modes[:, 1]
    )
    imag_part = mode_outer(coefficients[:, 0], sens_modes[:, 1]) - mode_outer(
        coefficients[:, 1], sens_modes[:, 0]
    )
    return jnp.stack([real_part, imag_part], axis=0)


def convolve(padded, kernel, cells_x):
    result = jnp.einsum("tcxs,cd->tdxs", padded[:, :, 0:cells_x], kernel[0], precision=HIGHEST)
    for offset in range(1, 3):
        result = result + jnp.einsum(
            "tcxs,cd->tdxs",
            padded[:, :, offset : offset + cells_x],
            kernel[offset],
            precision=HIGHEST,
        )
    return result


def convolve_adjoint(sens_padded, kernel, cells_x):
    result = jnp.einsum(
        "tdxs,cd->tcxs", sens_padded[:, :, 2 : 2 + cells_x], kernel[0], precision=HIGHEST
    )
    for offset in range(1, 3):
        result = result + jnp.einsum(
            "tdxs,cd->tcxs",
            sens_padded[:, :, 2 - offset : 2 - offset + cells_x],
            kernel[offset],
            precision=HIGHEST,
        )
    return result


def gelu_exact(values):
    return jax.nn.gelu(values, approximate=False)


def on_device(input_field, cotangent, spectral_weights, conv_kernel, mode_list):
    groups = lax.axis_size("tm")
    total_time = input_field.shape[0] * groups
    layers = conv_kernel.shape[0]
    factor = 2.0 / total_time
    cosine_all, sine_all = tables(mode_list, total_time, total_time)
    state_field, gradient = (input_field, cotangent)
    time_local, channels, cells_x, cells_s = state_field.shape
    cell_count = cells_x * cells_s
    saved = []
    for layer_number in range(layers):
        padded = extended(state_field, (("space", 2),), 1)
        convolved = convolve(padded, conv_kernel[layer_number], cells_x)
        flattened = state_field.reshape(time_local, channels, cell_count)
        series_field = lax.all_to_all(flattened, "tm", split_axis=2, concat_axis=0, tiled=True)
        coefficients = forward_dft(cosine_all, sine_all, series_field)
        mixed = channel_mix(coefficients, spectral_weights[layer_number])
        returned = inverse_dft(cosine_all, sine_all, mixed, factor)
        spectral_part = lax.all_to_all(returned, "tm", split_axis=0, concat_axis=2, tiled=True)
        preact = spectral_part.reshape(state_field.shape) + convolved
        saved.append((padded, coefficients, preact))
        state_field = gelu_exact(preact)
    kernel_pieces = []
    mode_pieces = []
    for layer_number in reversed(range(layers)):
        padded, coefficients, preact = saved[layer_number]
        pullback = jax.vjp(gelu_exact, preact)[1]
        sensitivity = pullback(gradient)[0]
        kernel_piece = jnp.stack(
            [
                jnp.einsum(
                    "tcxs,tdxs->cd",
                    padded[:, :, offset : offset + cells_x],
                    sensitivity,
                    precision=HIGHEST,
                )
                for offset in range(3)
            ]
        )
        sens_padded = extended(sensitivity, (("space", 2),), 1)
        back_conv = convolve_adjoint(sens_padded, conv_kernel[layer_number], cells_x)
        flat_sens = sensitivity.reshape(time_local, channels, cell_count)
        series_sens = lax.all_to_all(flat_sens, "tm", split_axis=2, concat_axis=0, tiled=True)
        sens_modes = factor * forward_dft(cosine_all, sine_all, series_sens)
        mode_piece = weight_grad(coefficients, sens_modes)
        adjoint = channel_mix_adjoint(sens_modes, spectral_weights[layer_number])
        returned = inverse_dft(cosine_all, sine_all, adjoint, 1.0)
        back_spec = lax.all_to_all(returned, "tm", split_axis=0, concat_axis=2, tiled=True)
        gradient = back_spec.reshape(sensitivity.shape) + back_conv
        kernel_pieces.append(kernel_piece)
        mode_pieces.append(mode_piece)
    kernel_total = lax.psum(jnp.stack(kernel_pieces[::-1]), ("tm", "space"))
    mode_stack = lax.psum_scatter(
        jnp.stack(mode_pieces[::-1]), "tm", scatter_dimension=2, tiled=True
    )
    mode_total = lax.psum(mode_stack, "space")
    return (gradient, mode_total, kernel_total)


def solution(mesh):
    placed = (P("tm", None, "space", None), P("tm", None, "space", None), P(), P(), P())
    return jax.shard_map(
        on_device,
        mesh=mesh,
        in_specs=placed,
        out_specs=(P("tm", None, "space", None), P(None, None, "tm", None, None), P()),
        check_vma=False,
    )
```

profile of v0, /device:TPU:0, one launch (start us, length us, event | category | flops | bytes accessed | tf_op | source)
XLA Modules:
  0.0 852.2 jit_solution(5890445966441035744)
XLA Ops:
  7.2 7.8 copy.219
  14.9 8.5 reshape.161
  23.4 33.1 %all_to_all.120 = f32[16,1,32768]{2,1,0:T(1,128)} all-to-all(f32[16,1,32768]{2,1,0:T(1,128)S(1)} %reshape.161), channel_id=1, replica_groups=mesh['tm'=16,'space'=8] {'tm'}, dimensions={0} | all-to-all | bytes 4194304 | tf_op jit(solution)/shard_map/all_to_all | solution.py:136
  57.0 7.3 reduce
  64.3 6.4 reshape.162
  70.7 6.9 copy.330
  92.8 4.6 all-to-all-start.1
  98.3 4.8 collective-permute-start
  104.6 4.3 fusion.154
  108.9 23.0 %collective-permute-done = f32[4,32,1,1024]{3,1,2,0:T(8,128)S(1)} collective-permute-done((f32[4,32,1,1024]{3,1,2,0:T(8,128)S(1)}, f32[4,32,1,1024]{3,1,2,0:T(8,128)S(1)}, u32[]{:S(2)}, u32[]{:S(2)}) %collective-permute-start) | collective-permute-done | bytes 524320 | tf_op jit(solution)/shard_map/ppermute | solution.py:18
  134.9 11.6 %collective-permute-done.1 = f32[4,32,1,1024]{3,1,2,0:T(8,128)S(1)} collective-permute-done((f32[4,32,1,1024]{3,1,2,0:T(8,128)S(1)}, f32[4,32,1,1024]{3,1,2,0:T(8,128)S(1)}, u32[]{:S(2)}, u32[]{:S(2)}) %collective-permute-start.1) | collective-permute-done | bytes 524320 | tf_op jit(solution)/shard_map/ppermute | solution.py:19
  155.9 10.0 %multiply_multiply_fusion.10 = (f32[4,32,4,1024]{3,1,2,0:T(8,128)S(1)}, f32[4,32,4,1024]{3,1,2,0:T(8,128)}) fusion(f32[4,32,5,1024]{3,1,2,0:T(8,128)} %constant_dynamic-update-slice_fusion.2, f32[2,3,32,32]{3,2,1,0:T(8,128)S(1)} %copy-done.28, f32[32,4,4,1024]{3,0,2,1:T(8,128)} %fusion.154, f32[4,4,1024,32]{2,3,1,0:T(8,128)} %fusion.157, ...), kind=kOutput, calls=%fused_computation.86 | convolution fusion | flops 236453888 | bytes 13123584 | tf_op jit(solution)/shard_map/tcxs,cd->tdxs/dot_general | solution.py:95
  165.9 5.9 copy.331
  171.8 9.5 %reshape.163 = f32[16,1,32768]{2,1,0:T(1,128)} reshape(f32[4096,4,32]{2,1,0:T(4,128)} %bitcast.414) | data formatting | bytes 4194304
  181.3 32.7 %all_to_all.121 = f32[16,1,32768]{2,1,0:T(1,128)} all-to-all(f32[16,1,32768]{2,1,0:T(1,128)} %reshape.163), channel_id=1, replica_groups=mesh['tm'=16,'space'=8] {'tm'}, dimensions={0} | all-to-all | bytes 4194304 | tf_op jit(solution)/shard_map/all_to_all | solution.py:136
  214.0 8.6 %reduce.1 = f32[16,32768]{1,0:T(8,128)} reduce(f32[16,1,32768]{2,1,0:T(1,128)} %all_to_all.121, f32[]{:T(128)} %broadcast.353), dimensions={1}, to_apply=%all_to_all.94.reduce_sub_computation | reduce | bytes 4194308 | tf_op jit(solution)/shard_map/all_to_all | solution.py:136
  222.6 7.7 reshape.164
  230.3 8.4 copy.239
  238.7 4.0 fusion.33
  255.3 4.4 all-to-all-start.3
  260.7 5.1 collective-permute-start.2
  270.5 23.8 %collective-permute-done.2 = f32[4,32,1,1024]{3,1,2,0:T(8,128)S(1)} collective-permute-done((f32[4,32,1,1024]{3,1,2,0:T(8,128)S(1)}, f32[4,32,1,1024]{3,1,2,0:T(8,128)S(1)}, u32[]{:S(2)}, u32[]{:S(2)}) %collective-permute-start.2) | collective-permute-done | bytes 524320 | tf_op jit(solution)/shard_map/ppermute | solution.py:18
  298.5 4.2 copy.245
  309.3 10.8 %fusion.26 = f32[4,32,4,1024]{3,1,2,0:T(8,128)} fusion(f32[4,32,4,1024]{3,2,1,0:T(4,128)} %param.6, f32[4,4,1024,32]{2,3,1,0:T(8,128)} %fusion.20, f32[4,4,1024,32]{2,3,1,0:T(8,128)} %fusion.142, f32[4,32,4,1024]{3,2,1,0:T(4,128)} %reshape.128, f32[4,32,1,1024]{3,1,2,0:T(8,128)} %collective-permute-done.3, f32[4,32,4,1024]{3,1,2,0:T(8,128)S(1)} %get-tuple-element.29, ...), kind=kOutput, calls=%fused_computation.38 | convolution fusion | flops 240779264 | bytes 13123584 | tf_op jit(solution)/shard_map/tcxs,cd->tdxs/dot_general | solution.py:95
  320.1 7.8 copy.332
  328.0 9.5 %reshape.165 = f32[16,1,32768]{2,1,0:T(1,128)} reshape(f32[4096,4,32]{2,1,0:T(4,128)} %bitcast.415) | data formatting | bytes 4194304
  337.5 32.9 %all_to_all.122 = f32[16,1,32768]{2,1,0:T(1,128)} all-to-all(f32[16,1,32768]{2,1,0:T(1,128)} %reshape.165), channel_id=1, replica_groups=mesh['tm'=16,'space'=8] {'tm'}, dimensions={0} | all-to-all | bytes 4194304 | tf_op jit(solution)/shard_map/all_to_all | solution.py:164
  370.4 8.6 %reduce.2 = f32[16,32768]{1,0:T(8,128)} reduce(f32[16,1,32768]{2,1,0:T(1,128)} %all_to_all.122, f32[]{:T(128)} %broadcast.353), dimensions={1}, to_apply=%all_to_all.100.reduce_sub_computation | reduce | bytes 4194308 | tf_op jit(solution)/shard_map/all_to_all | solution.py:164
  379.0 7.7 reshape.166
  386.7 8.4 copy.254
  412.7 4.6 all-to-all-start.5
  421.4 6.8 collective-permute-start.5
  438.2 17.2 %collective-permute-done.4 = f32[4,32,1,1024]{3,1,2,0:T(8,128)S(1)} collective-permute-done((f32[4,32,1,1024]{3,1,2,0:T(8,128)S(1)}, f32[4,32,1,1024]{3,1,2,0:T(8,128)S(1)}, u32[]{:S(2)}, u32[]{:S(2)}) %collective-permute-start.4) | collective-permute-done | bytes 524320 | tf_op jit(solution)/shard_map/ppermute | solution.py:19
  464.0 9.6 %multiply_add_fusion = f32[4,32,4,1024]{3,1,2,0:T(8,128)S(1)} fusion(f32[4,32,4,1024]{3,2,1,0:T(4,128)} %reshape.133, f32[4,4,1024,32]{2,3,1,0:T(8,128)} %fusion.2, f32[4,4,1024,32]{2,3,1,0:T(8,128)} %fusion.140, f32[4,32,4,1024]{3,1,2,0:T(8,128)} %get-tuple-element.30, f32[4,32,4,1024]{3,1,2,0:T(8,128)} %fusion.26, ...), kind=kOutput, calls=%fused_computation.57 | convolution fusion | flops 240779264 | bytes 13123584 | tf_op jit(solution)/shard_map/tdxs,cd->tcxs/dot_general | solution.py:109
  473.6 5.9 copy.336
  479.6 9.5 %reshape.167 = f32[16,1,32768]{2,1,0:T(1,128)} reshape(f32[4096,4,32]{2,1,0:T(4,128)} %bitcast.416) | data formatting | bytes 4194304
  489.0 5.1 all-to-all-start.6
  504.0 7.3 collective-permute-start.7
  522.0 8.6 %reduce.3 = f32[16,32768]{1,0:T(8,128)} reduce(f32[16,1,32768]{2,1,0:T(1,128)} %all-to-all-done.6, f32[]{:T(128)} %broadcast.353), dimensions={1}, to_apply=%all_to_all.106.reduce_sub_computation | reduce | bytes 4194308 | tf_op jit(solution)/shard_map/all_to_all | solution.py:164
  530.6 7.7 reshape.168
  538.3 8.1 copy.272
  564.1 5.3 all-to-all-start.7
  569.6 88.0 %psum.15 = f32[2,3,32,32]{3,2,1,0:T(8,128)} all-reduce(f32[2,3,32,32]{3,2,1,0:T(8,128)S(1)} %pad_maximum_fusion.11), channel_id=1, replica_groups=mesh['tm'=16,'space'=8] {'tm','space'}, use_global_device_ids=true, to_apply=%region_2.3 | all-reduce | flops 6144 | bytes 49152 | tf_op jit(solution)/shard_map/psum | solution.py:173
  666.6 4.5 fusion.10
  671.1 112.7 %all-reduce.3.cloned.1.call-done = f32[2,2,16,32,32]{4,3,2,1,0:T(8,128)} async-done(((f32[2,2,16,32,32]{4,3,2,1,0:T(8,128)}), f32[2,2,16,32,32]{4,3,2,1,0:T(8,128)}) %all-reduce.3.cloned.1.call-update) | async-done | bytes 262160
  785.1 43.4 %psum.14 = f32[2,2,1,32,32]{4,3,2,1,0:T(8,128)} all-reduce(f32[2,2,1,32,32]{4,3,2,1,0:T(8,128)S(1)} %constant_dynamic-slice_fusion), channel_id=1, replica_groups=mesh['tm'=16,'space'=8] {'space'}, use_global_device_ids=true, to_apply=%region_1.2 | all-reduce | flops 4096 | bytes 32768 | tf_op jit(solution)/shard_map/psum | solution.py:177
  828.5 4.1 copy.283
  835.8 6.4 bitcast_add_fusion
  (182 shorter events, 153.3 us)
Async XLA Ops:
  77.6 1.2 copy-start.30
  81.2 5.9 copy-start.11
  81.2 1.4 copy-start.6
  82.6 2.2 copy-start.7
  92.8 4.6 copy-start.1
  92.8 58.0 %all-to-all-start.1 = ((f32[64,32,256]{2,1,0:T(8,128)}), f32[64,32,256]{2,1,0:T(8,128)}, u32[]{:S(2)}, u32[]{:S(2)}) async-start(f32[64,32,256]{2,1,0:T(8,128)} %bitcast.439), calls=%async_computation.1 | async-start | bytes 4194304 | tf_op jit(solution)/shard_map/all_to_all | solution.py:140
  97.4 7.2 copy-start.28
  98.3 33.6 %collective-permute-start = (f32[4,32,1,1024]{3,1,2,0:T(8,128)S(1)}, f32[4,32,1,1024]{3,1,2,0:T(8,128)S(1)}, u32[]{:S(2)}, u32[]{:S(2)}) collective-permute-start(f32[4,32,1,1024]{3,1,2,0:T(8,128)S(1)} %copy.463), channel_id=1, source_target_pairs={{0,1},{1,2},{2,3},{3,4},{4,5},{5,6},{6,7},{8,9},{9,10},{10,11},{11... | collective-permute-start | bytes 1572872 | tf_op jit(solution)/shard_map/ppermute | solution.py:18
  103.2 43.2 %collective-permute-start.1 = (f32[4,32,1,1024]{3,1,2,0:T(8,128)S(1)}, f32[4,32,1,1024]{3,1,2,0:T(8,128)S(1)}, u32[]{:S(2)}, u32[]{:S(2)}) collective-permute-start(f32[4,32,1,1024]{3,1,2,0:T(8,128)S(1)} %copy.464), channel_id=1, source_target_pairs={{1,0},{2,1},{3,2},{4,3},{5,4},{6,5},{7,6},{9,8},{10,9},{11,10},{12... | collective-permute-start | bytes 1572872 | tf_op jit(solution)/shard_map/ppermute | solution.py:19
  134.9 12.5 %copy-start.23 = (f32[4,32,5,1024]{3,1,2,0:T(8,128)}, f32[4,32,5,1024]{3,1,2,0:T(8,128)S(1)}, u32[]{:S(2)}) copy-start(f32[4,32,5,1024]{3,1,2,0:T(8,128)S(1)} %get-tuple-element.24) | copy-start | bytes 7864324
  238.7 4.0 copy-start.3
  242.7 7.1 copy-start.13
  246.2 1.6 copy-start.9
  255.3 43.1 %all-to-all-start.3 = ((f32[64,32,256]{2,1,0:T(8,128)}), f32[64,32,256]{2,1,0:T(8,128)}, u32[]{:S(2)}, u32[]{:S(2)}) async-start(f32[64,32,256]{2,1,0:T(8,128)} %bitcast.440), calls=%async_computation.3 | async-start | bytes 4194304 | tf_op jit(solution)/shard_map/all_to_all | solution.py:140
  260.7 33.6 %collective-permute-start.2 = (f32[4,32,1,1024]{3,1,2,0:T(8,128)S(1)}, f32[4,32,1,1024]{3,1,2,0:T(8,128)S(1)}, u32[]{:S(2)}, u32[]{:S(2)}) collective-permute-start(f32[4,32,1,1024]{3,1,2,0:T(8,128)S(1)} %get-tuple-element.20), channel_id=1, source_target_pairs={{0,1},{1,2},{2,3},{3,4},{4,5},{5,6},{6,7},{8,9},{9,10},{10,11},{11... | collective-permute-start | bytes 1572872 | tf_op jit(solution)/shard_map/ppermute | solution.py:18
  265.8 43.5 %collective-permute-start.3 = (f32[4,32,1,1024]{3,1,2,0:T(8,128)}, f32[4,32,1,1024]{3,1,2,0:T(8,128)}, u32[]{:S(2)}, u32[]{:S(2)}) collective-permute-start(f32[4,32,1,1024]{3,1,2,0:T(8,128)} %get-tuple-element.19), channel_id=1, source_target_pairs={{1,0},{2,1},{3,2},{4,3},{5,4},{6,5},{7,6},{9,8},{10,9},{11,10},{12... | collective-permute-start | bytes 1572872 | tf_op jit(solution)/shard_map/ppermute | solution.py:19
  294.3 0.8 copy-start.25
  395.1 2.9 copy-start.4
  402.2 2.8 copy-start.15
  402.2 5.1 copy-start.17
  412.7 4.6 copy-start.32
  412.7 46.2 %all-to-all-start.5 = ((f32[64,32,256]{2,1,0:T(8,128)}), f32[64,32,256]{2,1,0:T(8,128)}, u32[]{:S(2)}, u32[]{:S(2)}) async-start(f32[64,32,256]{2,1,0:T(8,128)} %bitcast.438), calls=%async_computation.5 | async-start | bytes 4194304 | tf_op jit(solution)/shard_map/all_to_all | solution.py:169
  417.3 10.9 %copy-start = (f32[4,32,4,1024]{3,1,2,0:T(8,128)S(1)}, f32[4,32,4,1024]{3,1,2,0:T(8,128)}, u32[]{:S(2)}) copy-start(f32[4,32,4,1024]{3,1,2,0:T(8,128)} %fusion.26) | copy-start | bytes 6291460
  420.1 35.4 %collective-permute-start.4 = (f32[4,32,1,1024]{3,1,2,0:T(8,128)S(1)}, f32[4,32,1,1024]{3,1,2,0:T(8,128)S(1)}, u32[]{:S(2)}, u32[]{:S(2)}) collective-permute-start(f32[4,32,1,1024]{3,1,2,0:T(8,128)S(1)} %get-tuple-element.18), channel_id=1, source_target_pairs={{1,0},{2,1},{3,2},{4,3},{5,4},{6,5},{7,6},{9,8},{10,9},{11,10},{12... | collective-permute-start | bytes 1572872 | tf_op jit(solution)/shard_map/ppermute | solution.py:19
  421.4 42.6 %collective-permute-start.5 = (f32[4,32,1,1024]{3,1,2,0:T(8,128)}, f32[4,32,1,1024]{3,1,2,0:T(8,128)}, u32[]{:S(2)}, u32[]{:S(2)}) collective-permute-start(f32[4,32,1,1024]{3,1,2,0:T(8,128)} %get-tuple-element.17), channel_id=1, source_target_pairs={{0,1},{1,2},{2,3},{3,4},{4,5},{5,6},{6,7},{8,9},{9,10},{10,11},{11... | collective-permute-start | bytes 1572872 | tf_op jit(solution)/shard_map/ppermute | solution.py:18
  431.1 1.8 copy-start.26
  489.0 33.0 %all-to-all-start.6 = ((f32[16,1,32768]{2,1,0:T(1,128)}), f32[16,1,32768]{2,1,0:T(1,128)}, u32[]{:S(2)}, u32[]{:S(2)}) async-start(f32[16,1,32768]{2,1,0:T(1,128)} %reshape.167), calls=%async_computation.6 | async-start | bytes 4194304 | tf_op jit(solution)/shard_map/all_to_all | solution.py:164
  494.2 4.6 copy-start.14
  494.2 4.6 copy-start.18
  494.2 5.8 copy-start.10
  494.2 5.8 copy-start.16
  500.1 11.2 %copy-start.2 = (f32[4,32,4,1024]{3,2,1,0:T(4,128)S(1)}, f32[4,32,4,1024]{3,2,1,0:T(4,128)}, u32[]{:S(2)}) copy-start(f32[4,32,4,1024]{3,2,1,0:T(4,128)} %param.5) | copy-start | bytes 6291460
  502.7 163.9 %collective-permute-start.6 = (f32[4,32,1,1024]{3,1,2,0:T(8,128)}, f32[4,32,1,1024]{3,1,2,0:T(8,128)}, u32[]{:S(2)}, u32[]{:S(2)}) collective-permute-start(f32[4,32,1,1024]{3,1,2,0:T(8,128)} %get-tuple-element.16), channel_id=1, source_target_pairs={{1,0},{2,1},{3,2},{4,3},{5,4},{6,5},{7,6},{9,8},{10,9},{11,10},{12... | collective-permute-start | bytes 1572872 | tf_op jit(solution)/shard_map/ppermute | solution.py:19
  504.0 331.9 %collective-permute-start.7 = (f32[4,32,1,1024]{3,1,2,0:T(8,128)}, f32[4,32,1,1024]{3,1,2,0:T(8,128)}, u32[]{:S(2)}, u32[]{:S(2)}) collective-permute-start(f32[4,32,1,1024]{3,1,2,0:T(8,128)} %get-tuple-element.15), channel_id=1, source_target_pairs={{0,1},{1,2},{2,3},{3,4},{4,5},{5,6},{6,7},{8,9},{9,10},{10,11},{11... | collective-permute-start | bytes 1572872 | tf_op jit(solution)/shard_map/ppermute | solution.py:18
  514.1 3.6 copy-start.24
  546.5 3.0 copy-start.5
  546.5 3.0 copy-start.31
  553.6 2.8 copy-start.19
  553.6 5.1 copy-start.21
  564.1 5.4 copy-start.29
  564.1 264.4 %all-to-all-start.7 = ((f32[64,32,256]{2,1,0:T(8,128)}), f32[64,32,256]{2,1,0:T(8,128)}, u32[]{:S(2)}, u32[]{:S(2)}) async-start(f32[64,32,256]{2,1,0:T(8,128)} %bitcast.437), calls=%async_computation.7 | async-start | bytes 4194304 | tf_op jit(solution)/shard_map/all_to_all | solution.py:169
  569.5 214.2 %all-reduce.3.cloned.1.call-start = ((), (), s32[]{:S(2)}) async-start(), calls=%async_computation.8 | async-start | bytes 2097152
  657.6 3.5 copy-start.12
  657.6 3.5 copy-start.20
  657.6 4.7 copy-start.22
  661.0 2.4 copy-start.8
  662.2 3.0 copy-start.27
Sparse Core Ops, SparseCore 0:
  666.7 117.0 all-reduce.2
where the time goes:
time: 862 us; the launch traced here: 852 us
  blocking collectives  230 us (27%)
  waiting for transfers between devices  194 us (23%)
  local copies, waits for them, and re-layouts  186 us (22%)
  matrix products  138 us (16%)
  starting transfers between devices  53.3 us (6%)
  other arithmetic  35.2 us (4%)
  between operations  15.6 us (2%)
    unnamed x2, waiting for transfers between devices  113 us
    unnamed x102, local copies, waits for them, and re-layouts  103 us
    psum x1, blocking collectives, on_device(): kernel_total = lax.psum(jnp.stack(kernel_pieces[::-1]), ('tm', 'space'))  88 us
    all_to_all x2, blocking collectives, on_device(): lax.all_to_all(flattened, 'tm', split_axis=2, concat_axis=0, tiled=True)  65.8 us
    ppermute x4, waiting for transfers between devices, extended(): before = lax.ppermute(last, axis, up)  46.8 us
    psum x1, blocking collectives, on_device(): mode_total = lax.psum(mode_stack, 'space')  43.4 us
    all_to_all x1, blocking collectives, on_device(): lax.all_to_all(flat_sens, 'tm', split_axis=2, concat_axis=0, tiled=True)  32.9 us
    ppermute x4, waiting for transfers between devices, extended(): after = lax.ppermute(initial, axis, down)  32.3 us
  transfers between devices with their start and end apart: 14, of which 7 were waited for; matrix products, arithmetic and copies ran while one was open for 15% of the time, Pallas kernels for 0%

commit v1 on v0

v1 whole, which is shorter than its diff:
```python
import functools
import math

import jax
import jax.numpy as jnp
from jax import lax
from jax.experimental import pallas as pl
from jax.experimental.pallas import tpu as pltpu
from jax.sharding import PartitionSpec as P

F32 = jnp.float32
BF16 = jnp.bfloat16
LANES = 128
J = 8
XB = 4
C = 32
VMEM = pl.BlockSpec(memory_space=pltpu.VMEM)
PARAMS = pltpu.CompilerParams(vmem_limit_bytes=56 * 1024 * 1024)


def split(value):
    high = value.astype(BF16)
    low = (value - high.astype(F32)).astype(BF16)
    return high, low


def split_outside(value):
    high = lax.reduce_precision(value, 8, 7)
    return high.astype(BF16), (value - high).astype(BF16)


def dot3(left, right, dims=((1,), (0,))):
    (lh, ll), (rh, rl) = left, right
    (lc,), (rc,) = dims
    a = jnp.concatenate([lh, ll, lh], axis=lc)
    b = jnp.concatenate([rh, rh, rl], axis=rc)
    return lax.dot_general(a, b, (dims, ((), ())), preferred_element_type=F32)


def scatter_kernel(field_ref, out_ref):
    for q in range(field_ref.shape[3] // LANES):
        lanes = slice(q * LANES, (q + 1) * LANES)
        rows = jnp.concatenate([field_ref[0, :, x, lanes] for x in range(XB)], axis=0)
        groups = LANES // J
        out_ref[q * groups : (q + 1) * groups] = rows.T.reshape(groups, J, LANES)


def gather_kernel(blocks_ref, out_ref):
    groups = LANES // J
    for q in range(out_ref.shape[3] // LANES):
        lanes = slice(q * LANES, (q + 1) * LANES)
        rows = blocks_ref[q * groups : (q + 1) * groups].reshape(LANES, LANES).T
        for x in range(XB):
            out_ref[0, :, x, lanes] = rows[x * C : (x + 1) * C]


def to_blocks(field):
    steps, channels, cells, columns = field.shape
    parts = columns // J
    return pl.pallas_call(
        scatter_kernel,
        grid=(steps,),
        in_specs=[pl.BlockSpec((1, channels, cells, columns), lambda t: (t, 0, 0, 0))],
        out_specs=pl.BlockSpec((parts, J, LANES), lambda t: (0, t, 0)),
        out_shape=jax.ShapeDtypeStruct((parts, steps * J, LANES), F32),
        compiler_params=PARAMS,
    )(field)


def from_blocks(blocks):
    parts, rows, _ = blocks.shape
    steps = rows // J
    return pl.pallas_call(
        gather_kernel,
        grid=(steps,),
        in_specs=[pl.BlockSpec((parts, J, LANES), lambda t: (0, t, 0))],
        out_specs=pl.BlockSpec((1, C, XB, parts * J), lambda t: (t, 0, 0, 0)),
        out_shape=jax.ShapeDtypeStruct((steps, C, XB, parts * J), F32),
        compiler_params=PARAMS,
    )(blocks)


def tables(mode_list, total_time):
    def build(row_is_mode):
        modes, times = mode_list.shape[0], total_time
        shape = (modes * 2 * J, times * J) if row_is_mode else (times * J, modes * 2 * J)
        dm, dt = (0, 1) if row_is_mode else (1, 0)
        im = lax.broadcasted_iota(jnp.int32, shape, dm)
        it = lax.broadcasted_iota(jnp.int32, shape, dt)
        mode = jnp.repeat(mode_list, 2 * J, total_repeat_length=modes * 2 * J)
        mode = mode[:, None] if row_is_mode else mode[None, :]
        phase = (mode * (it // J)) % total_time
        angle = phase.astype(F32) * (2.0 * math.pi / total_time)
        value = jnp.where((im // J) % 2 == 0, jnp.cos(angle), -jnp.sin(angle))
        return split_outside(jnp.where(im % J == it % J, value, 0.0))

    return *build(True), *build(False)


def weights_kernel(scale, w_ref, high_ref, low_ref):
    modes = w_ref.shape[2]
    row = lax.broadcasted_iota(jnp.int32, (LANES, LANES), 0) // C
    col = lax.broadcasted_iota(jnp.int32, (LANES, LANES), 1) // C
    same = row == col

    def blocked(value):
        wide = jnp.concatenate([value] * XB, axis=1)
        return jnp.where(same, jnp.concatenate([wide] * XB, axis=0), 0.0)

    def body(m, _):
        re = split(blocked(w_ref[0, 0, m] * scale))
        im = split(blocked(w_ref[0, 1, m] * scale))
        for ref, r, i in ((high_ref, re[0], im[0]), (low_ref, re[1], im[1])):
            ref[0, m, :LANES, :LANES] = r
            ref[0, m, :LANES, LANES:] = i
            ref[0, m, LANES:, :LANES] = -i
            ref[0, m, LANES:, LANES:] = r
        return 0

    lax.fori_loop(0, modes, body, 0)


def block_weights(spectral_weights, scale):
    layers, _, modes, channels, _ = spectral_weights.shape
    out = jax.ShapeDtypeStruct((layers, modes, 2 * LANES, 2 * LANES), BF16)
    spec = pl.BlockSpec((1, modes, 2 * LANES, 2 * LANES), lambda l: (l, 0, 0, 0))
    return pl.pallas_call(
        functools.partial(weights_kernel, scale),
        grid=(layers,),
        in_specs=[
            pl.BlockSpec((1, 2, modes, channels, channels), lambda l: (l, 0, 0, 0, 0))
        ],
        out_specs=[spec, spec],
        out_shape=[out, out],
        compiler_params=PARAMS,
    )(spectral_weights)


def band(kernel):
    zero = jnp.zeros((C, C), F32)
    own = [
        [kernel[x - y + 1] if abs(x - y) <= 1 else zero for y in range(XB)] for x in range(XB)
    ]
    edge = [[zero] * XB for _ in range(XB)]
    edge[XB - 1][0] = kernel[0]
    edge[0][XB - 1] = kernel[2]
    return jnp.block(own + edge)


def bands(conv_kernel):
    forward = jnp.stack([band(k) for k in conv_kernel])
    adjoint = jnp.stack([band(jnp.swapaxes(k[::-1], 1, 2)) for k in conv_kernel])
    return *split_outside(forward), *split_outside(adjoint)


def lane_block():
    return lax.broadcasted_iota(jnp.int32, (1, LANES), 1) // C


def put_split(value, s, high_ref, low_ref):
    high, low = split(value)
    high_ref[s] = high
    low_ref[s] = low


def with_neighbours(ref, s):
    own = ref[s]
    x = lane_block()
    zero = jnp.zeros_like(own)
    before = ref[s - 1] if s > 0 else zero
    after = ref[s + 1] if s + 1 < ref.shape[0] else zero
    edge = jnp.where(x == XB - 1, before, jnp.where(x == 0, after, zero))
    return jnp.concatenate([own, edge], axis=1)


def analyse(table, high_ref, low_ref, coef_ref):
    for s in range(0, high_ref.shape[0], 2):
        right = [jnp.concatenate([r[s], r[s + 1]], axis=1) for r in (high_ref, low_ref)]
        result = dot3(table, right)
        coef_ref[s] = result[:, :LANES]
        coef_ref[s + 1] = result[:, LANES:]


def mix(coef_ref, wh_ref, wl_ref, l, mixed_ref, dims):
    bricks = coef_ref.shape[0]
    for m in range(wh_ref.shape[1]):
        re, im = slice(2 * J * m, 2 * J * m + J), slice(2 * J * m + J, 2 * J * (m + 1))
        value = jnp.concatenate(
            [coef_ref[:, re].reshape(bricks * J, LANES), coef_ref[:, im].reshape(bricks * J, LANES)],
            axis=1,
        )
        result = dot3(split(value), (wh_ref[l, m], wl_ref[l, m]), dims)
        mixed_ref[:, re] = result[:, :LANES].reshape(bricks, J, LANES)
        mixed_ref[:, im] = result[:, LANES:].reshape(bricks, J, LANES)


def synthesise(table, mixed_ref, bh, bl, high_ref, low_ref, emit):
    for s in range(0, mixed_ref.shape[0], 2):
        right = split(jnp.concatenate([mixed_ref[s], mixed_ref[s + 1]], axis=1))
        spectral = dot3(table, right)
        for o in range(2):
            value = (with_neighbours(high_ref, s + o), with_neighbours(low_ref, s + o))
            total = spectral[:, o * LANES : (o + 1) * LANES] + dot3(value, (bh, bl))
            emit(s + o, total)


def gelu_parts(z):
    cdf = 0.5 * (1.0 + lax.erf(z * math.sqrt(0.5)))
    slope = cdf + z * (jnp.exp(-0.5 * z * z) * (1.0 / math.sqrt(2.0 * math.pi)))
    return z * cdf, slope


def brick(ref, s):
    return ref[:, s].reshape(-1, LANES)


def forward_kernel(
    x_ref, ah, al, sh, sl, wh, wl, bh, bl,
    coef1, coef2, slope1, slope2, x1h, x1l, x2h, x2l, mixed,
):
    bricks = x_ref.shape[1]
    for s in range(bricks):
        put_split(brick(x_ref, s), s, x1h, x1l)
    analysis, synthesis = (ah[...], al[...]), (sh[...], sl[...])

    def first(s, z):
        value, slope = gelu_parts(z)
        slope1[s] = slope
        put_split(value, s, x2h, x2l)

    def second(s, z):
        slope2[s] = gelu_parts(z)[1]

    for l, (h, low, coef, emit) in enumerate(
        ((x1h, x1l, coef1, first), (x2h, x2l, coef2, second))
    ):
        analyse(analysis, h, low, coef)
        mix(coef, wh, wl, l, mixed, ((1,), (0,)))
        synthesise(synthesis, mixed, bh[l], bl[l], h, low, emit)


def forward(field, tabs, weights, bands_):
    _, bricks, _, _ = field.shape
    rows = tabs[0].shape[1]
    modes = tabs[0].shape[0]
    coef = jax.ShapeDtypeStruct((bricks, modes, LANES), F32)
    full = jax.ShapeDtypeStruct((bricks, rows, LANES), F32)
    half = jax.ShapeDtypeStruct((bricks, rows, LANES), BF16)
    return pl.pallas_call(
        forward_kernel,
        in_specs=[VMEM] * 9,
        out_specs=[VMEM] * 8,
        out_shape=[coef, coef, full, full, half, half, half, half],
        scratch_shapes=[pltpu.VMEM((bricks, modes, LANES), F32)],
        compiler_params=PARAMS,
    )(field, *tabs, *weights, *bands_[:2])


def backward_kernel(
    g_ref, slope1, slope2, ah, al, sh, sl, wh, wl, bh, bl,
    out_ref, sens1, sens2, z1h, z1l, z2h, z2l, mixed,
):
    bricks = g_ref.shape[1]
    for s in range(bricks):
        put_split(brick(g_ref, s) * slope2[s], s, z2h, z2l)
    analysis, synthesis = (ah[...], al[...]), (sh[...], sl[...])

    def second(s, g):
        put_split(g * slope1[s], s, z1h, z1l)

    def first(s, g):
        out_ref[:, s] = g.reshape(out_ref.shape[0], out_ref.shape[2], LANES)

    for l, (h, low, sens, emit) in ((1, (z2h, z2l, sens2, second)), (0, (z1h, z1l, sens1, first))):
        analyse(analysis, h, low, sens)
        mix(sens, wh, wl, l, mixed, ((1,), (1,)))
        synthesise(synthesis, mixed, bh[l], bl[l], h, low, emit)


def backward(cotangent, slope1, slope2, tabs, weights, bands_):
    _, bricks, _, _ = cotangent.shape
    rows = tabs[0].shape[1]
    modes = tabs[0].shape[0]
    coef = jax.ShapeDtypeStruct((bricks, modes, LANES), F32)
    half = jax.ShapeDtypeStruct((bricks, rows, LANES), BF16)
    return pl.pallas_call(
        backward_kernel,
        in_specs=[VMEM] * 11,
        out_specs=[VMEM] * 7,
        out_shape=[jax.ShapeDtypeStruct(cotangent.shape, F32), coef, coef, half, half, half, half],
        scratch_shapes=[pltpu.VMEM((bricks, modes, LANES), F32)],
        compiler_params=PARAMS,
    )(cotangent, slope1, slope2, *tabs, *weights, *bands_[2:])


ROWS = ((0,), (0,))


def weight_kernel(
    scale, coef1, coef2, sens1, sens2, x1h, x1l, x2h, x2l, z1h, z1l, z2h, z2l, out_ref
):
    bricks = coef1.shape[0]
    modes = coef1.shape[1] // (2 * J)
    for m in range(modes):
        re, im = slice(2 * J * m, 2 * J * m + J), slice(2 * J * m + J, 2 * J * (m + 1))
        pieces = []
        for coef, sens in ((coef1, sens1), (coef2, sens2)):
            cr, ci, zr, zi = (
                r[:, p].reshape(bricks * J, LANES)
                for r, p in ((coef, re), (coef, im), (sens, re), (sens, im))
            )
            left = jnp.concatenate([cr, ci], axis=0)
            right = jnp.concatenate(
                [jnp.concatenate([zr, zi], axis=1), jnp.concatenate([zi, -zr], axis=1)], axis=0
            )
            product = dot3(split(left), split(right), ROWS) * scale
            for part in range(2):
                pieces.append(
                    sum(
                        product[x * C : (x + 1) * C, part * LANES + x * C : part * LANES + (x + 1) * C]
                        for x in range(XB)
                    )
                )
        out_ref[m, :C] = jnp.concatenate(pieces, axis=1)
    lines = 2 * C // modes
    for l, (xh, xl, zh, zl) in enumerate(((x1h, x1l, z1h, z1l), (x2h, x2l, z2h, z2l))):
        total = jnp.zeros((LANES, 2 * LANES), F32)
        for s in range(bricks):
            value = (with_neighbours(xh, s), with_neighbours(xl, s))
            total = total + dot3((zh[s], zl[s]), value, ROWS)
        taps = []
        for j in range(3):
            pairs = [(x, x - j + 1) for x in range(XB) if 0 <= x - j + 1 < XB]
            tap = sum(total[y * C : (y + 1) * C, x * C : (x + 1) * C] for x, y in pairs)
            if j == 0:
                tap = tap + total[:C, LANES + (XB - 1) * C :]
            if j == 2:
                tap = tap + total[(XB - 1) * C :, LANES : LANES + C]
            taps.append(tap)
        wide = jnp.concatenate([*taps, jnp.zeros((C, C), F32)], axis=1)
        for i in range(modes // 2):
            out_ref[l * (modes // 2) + i, C : C + lines] = wide[i * lines : (i + 1) * lines]
    out_ref[:, C + lines :] = jnp.zeros((modes, out_ref.shape[1] - C - lines, LANES), F32)


def weight_gradients(scale, *operands):
    modes = operands[0].shape[1] // (2 * J)
    return pl.pallas_call(
        functools.partial(weight_kernel, scale),
        in_specs=[VMEM] * 12,
        out_specs=VMEM,
        out_shape=jax.ShapeDtypeStruct((modes, C + 8, LANES), F32),
        compiler_params=PARAMS,
    )(*operands)


def on_device(input_field, cotangent, spectral_weights, conv_kernel, mode_list):
    groups = lax.axis_size("tm")
    bricks = lax.axis_size("space")
    everyone = ("tm", "space")
    steps = input_field.shape[0]
    total_time = steps * groups
    layers, _, modes, _, _ = spectral_weights.shape
    scale = 2.0 / total_time
    exchange = functools.partial(lax.all_to_all, split_axis=0, concat_axis=0, tiled=True)

    received = exchange(to_blocks(input_field), everyone)
    cot_blocks = to_blocks(cotangent)
    tabs = tables(mode_list, total_time)
    weights = block_weights(spectral_weights, scale)
    bands_ = bands(conv_kernel)
    received, cot_blocks = lax.optimization_barrier((received, cot_blocks))
    cot_received = exchange(cot_blocks, everyone)
    shape = (groups, bricks, steps * J, LANES)
    coef1, coef2, slope1, slope2, x1h, x1l, x2h, x2l = forward(
        received.reshape(shape), tabs, weights, bands_
    )
    grad, sens1, sens2, z1h, z1l, z2h, z2l = backward(
        cot_received.reshape(shape), slope1, slope2, tabs, weights, bands_
    )
    returned = exchange(grad.reshape(cot_received.shape), everyone)
    partial = weight_gradients(
        scale, coef1, coef2, sens1, sens2, x1h, x1l, x2h, x2l, z1h, z1l, z2h, z2l
    )
    partial = reduce_over(partial, groups, "tm")
    spread = jnp.broadcast_to(partial[None], (bricks, *partial.shape))
    total = reduce_over(spread, bricks, "space")
    mode_total = total[:C].reshape(C, layers, 2, 1, C).transpose(1, 2, 3, 0, 4)
    lines = layers * C // groups
    own = total[C : C + lines]
    lined = exchange(jnp.broadcast_to(own[None], (groups, *own.shape)), "tm")
    kernel_total = lined.reshape(layers, C, LANES)[:, :, : 3 * C]
    kernel_total = kernel_total.reshape(layers, C, 3, C).transpose(0, 2, 3, 1)
    return (from_blocks(returned), mode_total, kernel_total)


def reduce_over(pieces, size, axis):
    got = lax.all_to_all(pieces, axis, split_axis=0, concat_axis=0, tiled=True)
    return jnp.sum(got.reshape(size, -1, LANES), axis=0)


def solution(mesh):
    placed = (P("tm", None, "space", None), P("tm", None, "space", None), P(), P(), P())
    return jax.shard_map(
        on_device,
        mesh=mesh,
        in_specs=placed,
        out_specs=(P("tm", None, "space", None), P(None, None, "tm", None, None), P()),
        check_vma=False,
    )
```

time: 862 us -> 203 us (0.24)
  blocking collectives: 230 us -> 36.9 us
  local copies, waits for them, and re-layouts: 186 us -> 6.59 us
  waiting for transfers between devices: 194 us -> 50.9 us
  matrix products: 138 us -> 0 us
  Pallas kernels: 0 us -> 63.6 us
  starting transfers between devices: 53.3 us -> 21.1 us
  other arithmetic: 35.2 us -> 20.1 us
  between operations: 15.6 us -> 0.9 us
    dot_general x58 -> x0, matrix products: 138 us -> none  [the longest x4 28.5 us: convolve(): jnp.einsum('tcxs,cd->tdxs', padded[:, :, offset:offset + cells_x], kernel...]
    psum x2 -> x0, blocking collectives: 131 us -> none  [the longest x1 88 us: on_device(): kernel_total = lax.psum(jnp.stack(kernel_pieces[::-1]), ('tm', 'space'))]
    unnamed x2 -> x0, waiting for transfers between devices: 113 us -> none
    unnamed x102 -> x16, local copies, waits for them, and re-layouts: 103 us -> 5.59 us
    ppermute x8 -> x0, waiting for transfers between devices: 79.1 us -> none  [the longest x4 46.8 us: extended(): before = lax.ppermute(last, axis, up)]
    pallas_call x0 -> x7, Pallas kernels: none -> 63.6 us  [the longest x1 18.1 us: backward(): pl.pallas_call(backward_kernel, in_specs=[VMEM] * 11, out_specs=[VMEM] *...]
    all_to_all x3, blocking collectives: 98.8 us -> 36.9 us  [the longest x2 28.3 us: reduce_over(): got = lax.all_to_all(pieces, axis, split_axis=0, concat_axis=0, tiled=True)]
    all_to_all x5 -> x3, waiting for transfers between devices: 1.84 us -> 50.9 us  [the longest x1 27.5 us: on_device(): returned = exchange(grad.reshape(cot_received.shape), everyone)]
  transfers between devices with their start and end apart: 14 -> 3, of which waited for: 7 -> 2; matrix products, arithmetic and copies ran while one was open for 15% -> 11% of each run, Pallas kernels for 0% -> 13%
where the time goes in v1:
time: 203 us; the launch traced here: 200 us
  Pallas kernels  63.6 us (31%)
  waiting for transfers between devices  50.9 us (25%)
  blocking collectives  36.9 us (18%)
  starting transfers between devices  21.1 us (10%)
  other arithmetic  20.1 us (10%)
  local copies, waits for them, and re-layouts  6.59 us (3%)
    all_to_all x2, blocking collectives, reduce_over(): got = lax.all_to_all(pieces, axis, split_axis=0, concat_axis=0, tiled=True)  28.3 us
    all_to_all x1, waiting for transfers between devices, on_device(): returned = exchange(grad.reshape(cot_received.shape), everyone)  27.5 us
    all_to_all x1, waiting for transfers between devices, on_device(): received = exchange(to_blocks(input_field), everyone)  23.3 us
    pallas_call x1, Pallas kernels, backward(): pl.pallas_call(backward_kernel, in_specs=[VMEM] * 11, out_specs=[VMEM] *...  18.1 us
    pallas_call x1, Pallas kernels, forward(): pl.pallas_call(forward_kernel, in_specs=[VMEM] * 9, out_specs=[VMEM] * 8,...  15.4 us
    all_to_all x1, starting transfers between devices, on_device(): received = exchange(to_blocks(input_field), everyone)  11.1 us
    select_n x1, other arithmetic, build(): mode = jnp.repeat(mode_list, 2 * J, total_repeat_length=modes * 2 * J)  9.99 us
    pallas_call x1, Pallas kernels, weight_gradients(): pl.pallas_call(functools.partial(weight_kernel, scale), in_specs=[VMEM] *...  9.54 us
  transfers between devices with their start and end apart: 3, of which 2 were waited for; matrix products, arithmetic and copies ran while one was open for 11% of the time, Pallas kernels for 13%

profile of v1, /device:TPU:0, one launch (start us, length us, event | category | flops | bytes accessed | tf_op | source)
XLA Modules:
  0.0 200.1 jit_solution(12831476899610141888)
XLA Ops:
  0.6 4.6 %shard_map.76 = f32[128,32,128]{2,1,0:T(8,128)} custom-call(f32[4,32,4,1024]{3,2,1,0:T(4,128)} %field_ref.2), custom_call_target="tpu_custom_call" | custom-call | tf_op jit(solution)/shard_map/pallas_call | solution.py:60
  5.2 11.1 %all-to-all-start = ((f32[128,32,128]{2,1,0:T(8,128)}), f32[128,32,128]{2,1,0:T(8,128)S(1)}, u32[]{:S(2)}, u32[]{:S(2)}) async-start(f32[128,32,128]{2,1,0:T(8,128)} %shard_map.76), calls=%async_computation | async-start | bytes 4194304 | tf_op jit(solution)/shard_map/all_to_all | solution.py:367
  16.5 0.1 copy.22
  16.7 4.5 %shard_map.77 = f32[128,32,128]{2,1,0:T(8,128)} custom-call(f32[4,32,4,1024]{3,2,1,0:T(4,128)} %field_ref.3), custom_call_target="tpu_custom_call" | custom-call | tf_op jit(solution)/shard_map/pallas_call | solution.py:60
  21.2 0.1 constant_dynamic-update-slice_fusion.23
  21.3 0.1 constant_dynamic-update-slice_fusion.22
  21.4 0.1 constant_dynamic-update-slice_fusion.21
  21.5 0.1 constant_dynamic-update-slice_fusion.20
  21.5 0.1 constant_dynamic-update-slice_fusion.19
  21.6 0.1 constant_dynamic-update-slice_fusion.18
  21.7 0.1 constant_dynamic-update-slice_fusion.30
  21.8 0.1 constant_dynamic-update-slice_fusion.17
  21.9 0.1 constant_dynamic-update-slice_fusion.14
  22.0 0.1 constant_dynamic-update-slice_fusion.16
  22.1 0.1 constant_dynamic-update-slice_fusion.27
  22.2 23.3 %all-to-all-done = f32[128,32,128]{2,1,0:T(8,128)S(1)} async-done(((f32[128,32,128]{2,1,0:T(8,128)}), f32[128,32,128]{2,1,0:T(8,128)S(1)}, u32[]{:S(2)}, u32[]{:S(2)}) %all-to-all-start) | async-done | bytes 2097184 | tf_op jit(solution)/shard_map/all_to_all | solution.py:367
  45.6 1.4 copy-done.2
  46.9 5.3 %all-to-all-start.1 = ((f32[128,32,128]{2,1,0:T(8,128)}), f32[128,32,128]{2,1,0:T(8,128)S(1)}, u32[]{:S(2)}, u32[]{:S(2)}) async-start(f32[128,32,128]{2,1,0:T(8,128)} %shard_map.77), calls=%async_computation.1 | async-start | bytes 4194304 | tf_op jit(solution)/shard_map/all_to_all | solution.py:373
  52.2 7.0 %shard_map.78 = (bf16[2,16,256,256]{3,2,1,0:T(8,128)(2,1)}, bf16[2,16,256,256]{3,2,1,0:T(8,128)(2,1)}) custom-call(f32[2,2,16,32,32]{4,3,2,1,0:T(8,128)} %w_ref.1), custom_call_target="tpu_custom_call" | custom-call | tf_op jit(solution)/shard_map/pallas_call | solution.py:127
  59.2 0.1 constant_dynamic-update-slice_fusion.26
  59.3 0.1 constant_dynamic-update-slice_fusion.5
  59.4 0.1 constant_dynamic-update-slice_fusion.4
  59.4 0.1 constant_dynamic-update-slice_fusion.25
  59.6 0.1 constant_dynamic-update-slice_fusion.2
  59.6 0.1 constant_dynamic-update-slice_fusion.24
  59.7 0.1 constant_dynamic-update-slice_fusion
  59.8 0.1 constant_dynamic-update-slice_fusion.8
  59.9 0.7 fusion.43
  60.6 0.7 fusion.13
  61.4 0.7 fusion.12
  62.1 10.0 %and_select_fusion = (s32[256]{0:T(256)S(1)}, s32[256]{0:T(256)S(1)}) fusion(s32[2,128]{1,0:T(2,128)S(1)} %copy-done.5, s32[]{:T(128)} %bitcast.18, s32[]{:T(128)} %bitcast.17, s32[]{:T(128)} %bitcast.16, s32[]{:T(128)} %bitcast.15, s32[]{:T(128)} %bitcast.14, s32[]{:T(128)} %bitcast.13, s32[]{:T(128)} %bitcast.12, s32[]{:T(128)} %bitcast.11, s32[]{:T(128)} %bitcast.10, ...), kind=kLoop, calls=%fused_computation.166 | loop fusion | flops 10240 | bytes 3144 | tf_op jit(solution)/shard_map/jit(_take)/select_n | solution.py:90
  72.1 3.6 %fusion.1 = (bf16[512,256]{1,0:T(8,128)(2,1)}, bf16[512,256]{1,0:T(8,128)(2,1)}) fusion(s32[512]{0:T(512)S(1)} %get-tuple-element.130, s32[512]{0:T(512)S(1)} %get-tuple-element.133, pred[512]{0:T(512)(128)(4,1)S(1)} %get-tuple-element.135, s32[256]{0:T(256)S(1)} %get-tuple-element.136, s32[256]{0:T(256)S(1)} %get-tuple-element.137, ...), kind=kLoop, calls=%fused_computation.21 | loop fusion | flops 4980736 | bytes 539136 | tf_op jit(solution)/shard_map/convert_element_type | solution.py:29
  75.7 3.3 %fusion = (bf16[256,512]{1,0:T(8,128)(2,1)}, bf16[256,512]{1,0:T(8,128)(2,1)}) fusion(s32[512]{0:T(512)S(1)} %get-tuple-element.130, s32[512]{0:T(512)S(1)} %get-tuple-element.133, pred[512]{0:T(512)(128)(4,1)S(1)} %get-tuple-element.135, s32[256]{0:T(256)S(1)} %get-tuple-element.136, s32[256]{0:T(256)S(1)} %get-tuple-element.137, ...), kind=kLoop, calls=%fused_computation.20 | loop fusion | flops 4980736 | bytes 539136 | tf_op jit(solution)/shard_map/convert_element_type | solution.py:29
  79.1 15.4 %shard_map.79 = (f32[8,256,128]{2,1,0:T(8,128)}, f32[8,256,128]{2,1,0:T(8,128)}, f32[8,512,128]{2,1,0:T(8,128)}, f32[8,512,128]{2,1,0:T(8,128)}, bf16[8,512,128]...) custom-call(f32[16,8,32,128]{3,2,1,0:T(8,128)} %bitcast.60, ...), custom_call_target="tpu_custom_call" | custom-call | tf_op jit(solution)/shard_map/pallas_call | solution.py:249
  94.5 1.3 copy-done
  95.8 18.1 %shard_map.80 = (f32[16,8,32,128]{3,2,1,0:T(8,128)}, f32[8,256,128]{2,1,0:T(8,128)}, f32[8,256,128]{2,1,0:T(8,128)}, bf16[8,512,128]{2,1,0:T(8,128)(2,1)}, bf16[...) custom-call(f32[16,8,32,128]{3,2,1,0:T(8,128)} %bitcast.59, ...), custom_call_target="tpu_custom_call" | custom-call | tf_op jit(solution)/shard_map/pallas_call | solution.py:286
  113.9 9.5 %shard_map.82 = f32[16,40,128]{2,1,0:T(8,128)} custom-call(f32[8,256,128]{2,1,0:T(8,128)} %get-tuple-element.51.coef1, f32[8,256,128]{2,1,0:T(8,128)} %get-tuple-element.52.coef2, f32[8,256,128]{2,1,0:T(8,128)} %get-tuple-element.53.sens1, f32[8,256,128]{2,1,0:T(8,128)} %get-tuple-element.54.sens2, bf16[8,512,128]{2,1,0:T(8,128)(2,1)} %get-tuple-element.55.x1h, ...), custom_call_target="tpu_custom_call" | custom-call | tf_op jit(solution)/shard_map/pallas_call | solution.py:348
  123.4 13.2 %all_to_all.30 = f32[16,40,128]{2,1,0:T(8,128)S(1)} all-to-all(f32[16,40,128]{2,1,0:T(8,128)} %shard_map.82), channel_id=1, replica_groups=mesh['tm'=16,'space'=8] {'tm'}, dimensions={0} | all-to-all | bytes 655360 | tf_op jit(solution)/shard_map/all_to_all | solution.py:398
  136.7 15.1 %all_to_all.31 = f32[8,40,128]{2,1,0:T(8,128)S(1)} all-to-all(f32[8,40,128]{2,1,0:T(8,128)S(1)} %broadcast_in_dim.32), channel_id=1, replica_groups=mesh['tm'=16,'space'=8] {'space'}, dimensions={0} | all-to-all | bytes 327680 | tf_op jit(solution)/shard_map/all_to_all | solution.py:398
  151.8 8.7 %all_to_all.32 = f32[16,4,128]{2,1,0:T(4,128)S(1)} all-to-all(f32[16,4,128]{2,1,0:T(4,128)S(1)} %broadcast_in_dim.33), channel_id=1, replica_groups=mesh['tm'=16,'space'=8] {'tm'}, dimensions={0} | all-to-all | bytes 65536 | tf_op jit(solution)/shard_map/all_to_all | solution.py:391
  160.5 4.6 %all-to-all-start.2 = ((f32[128,32,128]{2,1,0:T(8,128)}), f32[128,32,128]{2,1,0:T(8,128)S(1)}, u32[]{:S(2)}, u32[]{:S(2)}) async-start(f32[128,32,128]{2,1,0:T(8,128)} %bitcast.61), calls=%async_computation.2 | async-start | bytes 4194304 | tf_op jit(solution)/shard_map/all_to_all | solution.py:381
  165.1 0.1 reshape.98
  165.3 0.6 copy.20
  165.9 0.1 reshape.100
  166.0 0.7 copy.21
  166.7 27.5 %all-to-all-done.2.blocks_ref = f32[128,32,128]{2,1,0:T(8,128)S(1)} async-done(((f32[128,32,128]{2,1,0:T(8,128)}), f32[128,32,128]{2,1,0:T(8,128)S(1)}, u32[]{:S(2)}, u32[]{:S(2)}) %all-to-all-start.2) | async-done | bytes 2097184 | tf_op jit(solution)/shard_map/all_to_all | solution.py:381
  194.3 1.4 copy-done.1
  195.6 4.5 %shard_map.81 = f32[4,32,4,1024]{3,2,1,0:T(4,128)} custom-call(f32[128,32,128]{2,1,0:T(8,128)} %copy-done.1), custom_call_target="tpu_custom_call" | custom-call | tf_op jit(solution)/shard_map/pallas_call | solution.py:73
  (30 shorter events, 0.2 us)
Async XLA Ops:
  5.2 11.2 %copy-start.3 = (f32[2,3,32,32]{3,2,1,0:T(8,128)S(1)}, f32[2,3,32,32]{3,2,1,0:T(8,128)}, u32[]{:S(2)}) copy-start(f32[2,3,32,32]{3,2,1,0:T(8,128)} %param.46) | copy-start | bytes 73732
  5.2 40.3 %all-to-all-start = ((f32[128,32,128]{2,1,0:T(8,128)}), f32[128,32,128]{2,1,0:T(8,128)S(1)}, u32[]{:S(2)}, u32[]{:S(2)}) async-start(f32[128,32,128]{2,1,0:T(8,128)} %shard_map.76), calls=%async_computation | async-start | bytes 4194304 | tf_op jit(solution)/shard_map/all_to_all | solution.py:367
  22.2 37.7 %copy-start.4 = (s32[16]{0:T(128)S(1)}, s32[16]{0:T(128)}, u32[]{:S(2)}) copy-start(s32[16]{0:T(128)} %param.47) | copy-start | bytes 196
  45.6 1.4 copy-start.2
  46.9 47.6 %all-to-all-start.1 = ((f32[128,32,128]{2,1,0:T(8,128)}), f32[128,32,128]{2,1,0:T(8,128)S(1)}, u32[]{:S(2)}, u32[]{:S(2)}) async-start(f32[128,32,128]{2,1,0:T(8,128)} %shard_map.77), calls=%async_computation.1 | async-start | bytes 4194304 | tf_op jit(solution)/shard_map/all_to_all | solution.py:373
  52.2 9.9 %copy-start.5 = (s32[2,128]{1,0:T(2,128)S(1)}, s32[2,128]{1,0:T(2,128)}, u32[]{:S(2)}) copy-start(s32[2,128]{1,0:T(2,128)} %constant.194.clone.1) | copy-start | bytes 3076
  94.5 1.3 copy-start
  160.5 33.8 %all-to-all-start.2 = ((f32[128,32,128]{2,1,0:T(8,128)}), f32[128,32,128]{2,1,0:T(8,128)S(1)}, u32[]{:S(2)}, u32[]{:S(2)}) async-start(f32[128,32,128]{2,1,0:T(8,128)} %bitcast.61), calls=%async_computation.2 | async-start | bytes 4194304 | tf_op jit(solution)/shard_map/all_to_all | solution.py:381
  194.3 1.4 copy-start.1

commit v2 on v1

--- a/solution.py
+++ b/solution.py
@@ -294,10 +294,17 @@
 
 
 ROWS = ((0,), (0,))
+RADIX = 4
+
+
+def slot(place, owner):
+    low = (owner % RADIX - place[1] + RADIX) % RADIX
+    high = (owner // RADIX - place[0] + RADIX) % RADIX
+    return low * RADIX + high
 
 
 def weight_kernel(
-    scale, coef1, coef2, sens1, sens2, x1h, x1l, x2h, x2l, z1h, z1l, z2h, z2l, out_ref
+    scale, place, coef1, coef2, sens1, sens2, x1h, x1l, x2h, x2l, z1h, z1l, z2h, z2l, out_ref
 ):
     bricks = coef1.shape[0]
     modes = coef1.shape[1] // (2 * J)
@@ -321,7 +328,7 @@
                         for x in range(XB)
                     )
                 )
-        out_ref[m, :C] = jnp.concatenate(pieces, axis=1)
+        out_ref[slot(place, m), :C] = jnp.concatenate(pieces, axis=1)
     lines = 2 * C // modes
     for l, (xh, xl, zh, zl) in enumerate(((x1h, x1l, z1h, z1l), (x2h, x2l, z2h, z2l))):
         total = jnp.zeros((LANES, 2 * LANES), F32)
@@ -339,15 +346,16 @@
             taps.append(tap)
         wide = jnp.concatenate([*taps, jnp.zeros((C, C), F32)], axis=1)
         for i in range(modes // 2):
-            out_ref[l * (modes // 2) + i, C : C + lines] = wide[i * lines : (i + 1) * lines]
+            part = wide[i * lines : (i + 1) * lines]
+            out_ref[slot(place, l * (modes // 2) + i), C : C + lines] = part
     out_ref[:, C + lines :] = jnp.zeros((modes, out_ref.shape[1] - C - lines, LANES), F32)
 
 
 def weight_gradients(scale, *operands):
-    modes = operands[0].shape[1] // (2 * J)
+    modes = operands[1].shape[1] // (2 * J)
     return pl.pallas_call(
         functools.partial(weight_kernel, scale),
-        in_specs=[VMEM] * 12,
+        in_specs=[pl.BlockSpec(memory_space=pltpu.SMEM)] + [VMEM] * 12,
         out_specs=VMEM,
         out_shape=jax.ShapeDtypeStruct((modes, C + 8, LANES), F32),
         compiler_params=PARAMS,
@@ -369,7 +377,9 @@
     tabs = tables(mode_list, total_time)
     weights = block_weights(spectral_weights, scale)
     bands_ = bands(conv_kernel)
-    received, cot_blocks = lax.optimization_barrier((received, cot_blocks))
+    received, cot_blocks, tabs, weights, bands_ = lax.optimization_barrier(
+        (received, cot_blocks, tabs, weights, bands_)
+    )
     cot_received = exchange(cot_blocks, everyone)
     shape = (groups, bricks, steps * J, LANES)
     coef1, coef2, slope1, slope2, x1h, x1l, x2h, x2l = forward(
@@ -379,24 +389,37 @@
         cot_received.reshape(shape), slope1, slope2, tabs, weights, bands_
     )
     returned = exchange(grad.reshape(cot_received.shape), everyone)
+    me = lax.axis_index("tm")
+    place = jnp.stack([me // RADIX, me % RADIX]).astype(jnp.int32)
     partial = weight_gradients(
-        scale, coef1, coef2, sens1, sens2, x1h, x1l, x2h, x2l, z1h, z1l, z2h, z2l
+        scale, place, coef1, coef2, sens1, sens2, x1h, x1l, x2h, x2l, z1h, z1l, z2h, z2l
     )
-    partial = reduce_over(partial, groups, "tm")
-    spread = jnp.broadcast_to(partial[None], (bricks, *partial.shape))
-    total = reduce_over(spread, bricks, "space")
+    partial = partial.reshape(RADIX, RADIX, *partial.shape[1:])
+    partial = shifted_sum(list(partial), "tm", groups, 1)
+    partial = shifted_sum(list(partial), "tm", groups, RADIX)
+    partial = shifted_sum([partial] * RADIX, "space", bricks, bricks // RADIX)
+    total = shifted_sum([partial] * (bricks // RADIX), "space", bricks, 1)
     mode_total = total[:C].reshape(C, layers, 2, 1, C).transpose(1, 2, 3, 0, 4)
     lines = layers * C // groups
-    own = total[C : C + lines]
+    returned, own = lax.optimization_barrier((returned, total[C : C + lines]))
     lined = exchange(jnp.broadcast_to(own[None], (groups, *own.shape)), "tm")
     kernel_total = lined.reshape(layers, C, LANES)[:, :, : 3 * C]
     kernel_total = kernel_total.reshape(layers, C, 3, C).transpose(0, 2, 3, 1)
     return (from_blocks(returned), mode_total, kernel_total)
 
 
-def reduce_over(pieces, size, axis):
-    got = lax.all_to_all(pieces, axis, split_axis=0, concat_axis=0, tiled=True)
-    return jnp.sum(got.reshape(size, -1, LANES), axis=0)
+def shifted_sum(pieces, axis, size, stride):
+    count = len(pieces)
+    got = [pieces[0]]
+    for r in range(1, count):
+        perm = []
+        for i in range(size):
+            digit = i // stride % count
+            perm.append((i, i + ((digit + r) % count - digit) * stride))
+        got.append(lax.ppermute(pieces[r], axis, perm))
+    if count == 2:
+        return got[0] + got[1]
+    return (got[0] + got[2]) + (got[1] + got[3])
 
 
 def solution(mesh):

time: 203 us -> 178 us (0.88)
  blocking collectives: 36.9 us -> 0 us
  starting transfers between devices: 21.1 us -> 49.8 us
  waiting for transfers between devices: 50.9 us -> 32.9 us
    all_to_all x3 -> x0, blocking collectives: 36.9 us -> none  [the longest x2 28.3 us: reduce_over(): got = lax.all_to_all(pieces, axis, split_axis=0, concat_axis=0, tiled=True)]
    all_to_all x1, waiting for transfers between devices: 27.5 us -> 0.01 us  [on_device(): returned = exchange(grad.reshape(cot_received.shape), everyone)]
    all_to_all x1, waiting for transfers between devices: 23.3 us -> 0.01 us  [on_device(): received = exchange(to_blocks(input_field), everyone)]
    ppermute x0 -> x10, starting transfers between devices: none -> 18.8 us  [shifted_sum(): got.append(lax.ppermute(pieces[r], axis, perm))]
    ppermute x0 -> x10, waiting for transfers between devices: none -> 18.7 us  [shifted_sum(): got.append(lax.ppermute(pieces[r], axis, perm))]
    all_to_all x1, waiting for transfers between devices: 0.01 us -> 13.4 us  [on_device(): cot_received = exchange(cot_blocks, everyone)]
    all_to_all x1, starting transfers between devices: 5.26 us -> 9.94 us  [on_device(): cot_received = exchange(cot_blocks, everyone)]
    all_to_all x0 -> x1, starting transfers between devices: none -> 4.65 us  [on_device(): lined = exchange(jnp.broadcast_to(own[None], (groups, *own.shape)), 'tm')]
  transfers between devices with their start and end apart: 3 -> 14, of which waited for: 2 -> 7; matrix products, arithmetic and copies ran while one was open for 11% -> 14% of each run, Pallas kernels for 13% -> 23%
where the time goes in v2:
time: 178 us; the launch traced here: 176 us
  Pallas kernels  63.8 us (36%)
  starting transfers between devices  49.8 us (28%)
  waiting for transfers between devices  32.9 us (18%)
  other arithmetic  21.7 us (12%)
  local copies, waits for them, and re-layouts  6.81 us (4%)
    ppermute x10, starting transfers between devices, shifted_sum(): got.append(lax.ppermute(pieces[r], axis, perm))  18.8 us
    ppermute x10, waiting for transfers between devices, shifted_sum(): got.append(lax.ppermute(pieces[r], axis, perm))  18.7 us
    pallas_call x1, Pallas kernels, backward(): pl.pallas_call(backward_kernel, in_specs=[VMEM] * 11, out_specs=[VMEM] *...  18 us
    pallas_call x1, Pallas kernels, forward(): pl.pallas_call(forward_kernel, in_specs=[VMEM] * 9, out_specs=[VMEM] * 8,...  15.6 us
    all_to_all x1, waiting for transfers between devices, on_device(): cot_received = exchange(cot_blocks, everyone)  13.4 us
    all_to_all x1, starting transfers between devices, on_device(): received = exchange(to_blocks(input_field), everyone)  11.1 us
    select_n x1, other arithmetic, build(): mode = jnp.repeat(mode_list, 2 * J, total_repeat_length=modes * 2 * J)  10 us
    all_to_all x1, starting transfers between devices, on_device(): cot_received = exchange(cot_blocks, everyone)  9.94 us
  transfers between devices with their start and end apart: 14, of which 7 were waited for; matrix products, arithmetic and copies ran while one was open for 14% of the time, Pallas kernels for 23%

profile of v2, /device:TPU:0, one launch (start us, length us, event | category | flops | bytes accessed | tf_op | source)
XLA Modules:
  0.0 176.0 jit_solution(13058340616600914237)
XLA Ops:
  0.6 4.5 %shard_map.76 = f32[128,32,128]{2,1,0:T(8,128)} custom-call(f32[4,32,4,1024]{3,2,1,0:T(4,128)} %field_ref.2), custom_call_target="tpu_custom_call" | custom-call | tf_op jit(solution)/shard_map/pallas_call | solution.py:60
  5.2 11.1 %all-to-all-start = ((f32[128,32,128]{2,1,0:T(8,128)}), f32[128,32,128]{2,1,0:T(8,128)S(1)}, u32[]{:S(2)}, u32[]{:S(2)}) async-start(f32[128,32,128]{2,1,0:T(8,128)} %shard_map.76), calls=%async_computation | async-start | bytes 4194304 | tf_op jit(solution)/shard_map/all_to_all | solution.py:375
  17.1 0.1 constant_dynamic-update-slice_fusion.18
  17.3 0.1 constant_dynamic-update-slice_fusion.17
  17.5 0.1 constant_dynamic-update-slice_fusion.16
  17.7 6.9 %shard_map.78 = (bf16[2,16,256,256]{3,2,1,0:T(8,128)(2,1)}, bf16[2,16,256,256]{3,2,1,0:T(8,128)(2,1)}) custom-call(f32[2,2,16,32,32]{4,3,2,1,0:T(8,128)} %w_ref.1), custom_call_target="tpu_custom_call" | custom-call | tf_op jit(solution)/shard_map/pallas_call | solution.py:127
  24.6 4.5 %shard_map.77 = f32[128,32,128]{2,1,0:T(8,128)} custom-call(f32[4,32,4,1024]{3,2,1,0:T(4,128)} %field_ref.3), custom_call_target="tpu_custom_call" | custom-call | tf_op jit(solution)/shard_map/pallas_call | solution.py:60
  29.1 0.1 constant_dynamic-update-slice_fusion.26
  29.4 0.1 constant_dynamic-update-slice_fusion.25
  29.8 0.7 fusion.47
  30.6 0.7 fusion.13
  31.3 0.7 fusion.12
  32.1 10.0 %and_select_fusion = (s32[256]{0:T(256)S(1)}, s32[256]{0:T(256)S(1)}) fusion(s32[2,128]{1,0:T(2,128)S(1)} %copy-done.5, s32[]{:T(128)} %bitcast.16, s32[]{:T(128)} %bitcast.15, s32[]{:T(128)} %bitcast.14, s32[]{:T(128)} %bitcast.13, s32[]{:T(128)} %bitcast.12, s32[]{:T(128)} %bitcast.11, s32[]{:T(128)} %bitcast.10, s32[]{:T(128)} %bitcast.9, s32[]{:T(128)} %bitcast.8, ...), kind=kLoop, calls=%fused_computation.176 | loop fusion | flops 10240 | bytes 3144 | tf_op jit(solution)/shard_map/jit(_take)/select_n | solution.py:90
  42.1 3.6 %fusion.1 = (bf16[512,256]{1,0:T(8,128)(2,1)}, bf16[512,256]{1,0:T(8,128)(2,1)}) fusion(s32[512]{0:T(512)S(1)} %get-tuple-element.154, s32[512]{0:T(512)S(1)} %get-tuple-element.157, pred[512]{0:T(512)(128)(4,1)S(1)} %get-tuple-element.159, s32[256]{0:T(256)S(1)} %get-tuple-element.160, s32[256]{0:T(256)S(1)} %get-tuple-element.161, ...), kind=kLoop, calls=%fused_computation.21 | loop fusion | flops 4980736 | bytes 539136 | tf_op jit(solution)/shard_map/convert_element_type | solution.py:29
  45.7 3.3 %fusion = (bf16[256,512]{1,0:T(8,128)(2,1)}, bf16[256,512]{1,0:T(8,128)(2,1)}) fusion(s32[512]{0:T(512)S(1)} %get-tuple-element.154, s32[512]{0:T(512)S(1)} %get-tuple-element.157, pred[512]{0:T(512)(128)(4,1)S(1)} %get-tuple-element.159, s32[256]{0:T(256)S(1)} %get-tuple-element.160, s32[256]{0:T(256)S(1)} %get-tuple-element.161, ...), kind=kLoop, calls=%fused_computation.20 | loop fusion | flops 4980736 | bytes 539136 | tf_op jit(solution)/shard_map/convert_element_type | solution.py:29
  49.0 1.3 copy-done.2
  50.4 9.9 %all-to-all-start.1 = ((f32[128,32,128]{2,1,0:T(8,128)}), f32[128,32,128]{2,1,0:T(8,128)S(1)}, u32[]{:S(2)}, u32[]{:S(2)}) async-start(f32[128,32,128]{2,1,0:T(8,128)} %shard_map.77), calls=%async_computation.1 | async-start | bytes 4194304 | tf_op jit(solution)/shard_map/all_to_all | solution.py:383
  60.3 15.6 %shard_map.79 = (f32[8,256,128]{2,1,0:T(8,128)}, f32[8,256,128]{2,1,0:T(8,128)}, f32[8,512,128]{2,1,0:T(8,128)}, f32[8,512,128]{2,1,0:T(8,128)}, bf16[8,512,128]...) custom-call(f32[16,8,32,128]{3,2,1,0:T(8,128)} %bitcast.76, ...), custom_call_target="tpu_custom_call" | custom-call | tf_op jit(solution)/shard_map/pallas_call | solution.py:249
  75.9 13.4 %all-to-all-done.1 = f32[128,32,128]{2,1,0:T(8,128)S(1)} async-done(((f32[128,32,128]{2,1,0:T(8,128)}), f32[128,32,128]{2,1,0:T(8,128)S(1)}, u32[]{:S(2)}, u32[]{:S(2)}) %all-to-all-start.1) | async-done | bytes 2097184 | tf_op jit(solution)/shard_map/all_to_all | solution.py:383
  89.3 1.3 copy-done
  90.6 18.0 %shard_map.80 = (f32[16,8,32,128]{3,2,1,0:T(8,128)}, f32[8,256,128]{2,1,0:T(8,128)}, f32[8,256,128]{2,1,0:T(8,128)}, bf16[8,512,128]{2,1,0:T(8,128)(2,1)}, bf16[...) custom-call(f32[16,8,32,128]{3,2,1,0:T(8,128)} %bitcast.75, ...), custom_call_target="tpu_custom_call" | custom-call | tf_op jit(solution)/shard_map/pallas_call | solution.py:286
  108.6 5.3 %all-to-all-start.2 = ((f32[128,32,128]{2,1,0:T(8,128)}), f32[128,32,128]{2,1,0:T(8,128)S(1)}, u32[]{:S(2)}, u32[]{:S(2)}) async-start(f32[128,32,128]{2,1,0:T(8,128)} %bitcast.77), calls=%async_computation.2 | async-start | bytes 4194304 | tf_op jit(solution)/shard_map/all_to_all | solution.py:391
  113.9 0.6 pad_add_fusion.place
  114.5 9.7 %shard_map.81 = f32[16,40,128]{2,1,0:T(8,128)} custom-call(s32[2]{0:T(128)} %pad_add_fusion.place, f32[8,256,128]{2,1,0:T(8,128)} %get-tuple-element.73.coef1, f32[8,256,128]{2,1,0:T(8,128)} %get-tuple-element.74.coef2, f32[8,256,128]{2,1,0:T(8,128)} %get-tuple-element.75.sens1, f32[8,256,128]{2,1,0:T(8,128)} %get-tuple-element.76.sens2, ...), custom_call_target="tpu_custom_call" | custom-call | tf_op jit(solution)/shard_map/pallas_call | solution.py:356
  124.2 1.0 fusion.45
  125.2 1.0 collective-permute-start
  126.3 1.7 collective-permute-start.2
  128.0 11.9 %collective-permute-done = f32[4,40,128]{2,1,0:T(8,128)S(1)} collective-permute-done((f32[4,40,128]{2,1,0:T(8,128)S(1)}, f32[4,40,128]{2,1,0:T(8,128)S(1)}, u32[]{:S(2)}, u32[]{:S(2)}) %collective-permute-start) | collective-permute-done | bytes 81952 | tf_op jit(solution)/shard_map/ppermute | solution.py:419
  139.9 0.8 collective-permute-done.1
  140.7 0.9 fusion.14
  141.6 3.0 %collective-permute-start.3 = (f32[40,128]{1,0:T(8,128)S(1)}, f32[40,128]{1,0:T(8,128)S(1)}, u32[]{:S(2)}, u32[]{:S(2)}) collective-permute-start(f32[40,128]{1,0:T(8,128)S(1)} %get-tuple-element.107), channel_id=1, source_target_pairs={{0,64},{8,72},{16,80},{24,88},{32,96},{40,104},{48,112},{56,120},{... | collective-permute-start | bytes 61448 | tf_op jit(solution)/shard_map/ppermute | solution.py:419
  144.7 0.7 collective-permute-start.4
  145.4 2.5 %collective-permute-start.5 = (f32[40,128]{1,0:T(8,128)S(1)}, f32[40,128]{1,0:T(8,128)S(1)}, u32[]{:S(2)}, u32[]{:S(2)}) collective-permute-start(f32[40,128]{1,0:T(8,128)S(1)} %get-tuple-element.105), channel_id=1, source_target_pairs={{0,96},{8,104},{16,112},{24,120},{32,0},{40,8},{48,16},{56,24},{64... | collective-permute-start | bytes 61448 | tf_op jit(solution)/shard_map/ppermute | solution.py:419
  147.9 1.8 collective-permute-done.4
  149.7 3.6 %collective-permute-start.6 = (f32[40,128]{1,0:T(8,128)S(1)}, f32[40,128]{1,0:T(8,128)S(1)}, u32[]{:S(2)}, u32[]{:S(2)}) collective-permute-start(f32[40,128]{1,0:T(8,128)S(1)} %fusion.24), channel_id=1, source_target_pairs={{0,4},{1,5},{2,6},{3,7},{4,0},{5,1},{6,2},{7,3},{8,12},{9,13},{10,... | collective-permute-start | bytes 61448 | tf_op jit(solution)/shard_map/ppermute | solution.py:419
  153.3 0.8 collective-permute-start.7
  154.1 2.4 %collective-permute-start.8 = (f32[40,128]{1,0:T(8,128)S(1)}, f32[40,128]{1,0:T(8,128)S(1)}, u32[]{:S(2)}, u32[]{:S(2)}) collective-permute-start(f32[40,128]{1,0:T(8,128)S(1)} %fusion.24), channel_id=1, source_target_pairs={{0,6},{1,7},{2,0},{3,1},{4,2},{5,3},{6,4},{7,5},{8,14},{9,15},{10,... | collective-permute-start | bytes 61448 | tf_op jit(solution)/shard_map/ppermute | solution.py:419
  156.5 1.8 collective-permute-done.7
  158.3 2.9 %collective-permute-start.9 = (f32[40,128]{1,0:T(8,128)S(1)}, f32[40,128]{1,0:T(8,128)S(1)}, u32[]{:S(2)}, u32[]{:S(2)}) collective-permute-start(f32[40,128]{1,0:T(8,128)S(1)} %add_add_fusion), channel_id=1, source_target_pairs={{0,1},{1,0},{2,3},{3,2},{4,5},{5,4},{6,7},{7,6},{8,9},{9,8},{10,11... | collective-permute-start | bytes 61448 | tf_op jit(solution)/shard_map/ppermute | solution.py:419
  161.2 2.5 %collective-permute-done.9 = f32[40,128]{1,0:T(8,128)S(1)} collective-permute-done((f32[40,128]{1,0:T(8,128)S(1)}, f32[40,128]{1,0:T(8,128)S(1)}, u32[]{:S(2)}, u32[]{:S(2)}) %collective-permute-start.9) | collective-permute-done | bytes 20512 | tf_op jit(solution)/shard_map/ppermute | solution.py:419
  163.7 0.7 broadcast_in_dim.26
  164.4 4.6 %all-to-all-start.3 = ((f32[16,4,128]{2,1,0:T(4,128)}), f32[16,4,128]{2,1,0:T(4,128)S(1)}, u32[]{:S(2)}, u32[]{:S(2)}) async-start(f32[16,4,128]{2,1,0:T(4,128)} %broadcast_in_dim.26), calls=%async_computation.3 | async-start | bytes 65536 | tf_op jit(solution)/shard_map/all_to_all | solution.py:405
  169.0 0.1 reshape.106
  169.1 0.6 copy.22
  169.8 4.5 %shard_map.82 = f32[4,32,4,1024]{3,2,1,0:T(4,128)} custom-call(f32[128,32,128]{2,1,0:T(8,128)} %copy-done.1), custom_call_target="tpu_custom_call" | custom-call | tf_op jit(solution)/shard_map/pallas_call | solution.py:73
  174.3 0.9 all-to-all-done.3
  175.1 0.1 reshape.108
  175.3 0.7 copy.18
  (53 shorter events, 1.5 us)
Async XLA Ops:
  5.2 11.2 %copy-start.3 = (f32[2,3,32,32]{3,2,1,0:T(8,128)S(1)}, f32[2,3,32,32]{3,2,1,0:T(8,128)}, u32[]{:S(2)}) copy-start(f32[2,3,32,32]{3,2,1,0:T(8,128)} %param.46) | copy-start | bytes 73732
  5.2 43.9 %all-to-all-start = ((f32[128,32,128]{2,1,0:T(8,128)}), f32[128,32,128]{2,1,0:T(8,128)S(1)}, u32[]{:S(2)}, u32[]{:S(2)}) async-start(f32[128,32,128]{2,1,0:T(8,128)} %shard_map.76), calls=%async_computation | async-start | bytes 4194304 | tf_op jit(solution)/shard_map/all_to_all | solution.py:375
  24.6 5.2 %copy-start.4 = (s32[16]{0:T(128)S(1)}, s32[16]{0:T(128)}, u32[]{:S(2)}) copy-start(s32[16]{0:T(128)} %param.47) | copy-start | bytes 196
  24.6 7.5 %copy-start.5 = (s32[2,128]{1,0:T(2,128)S(1)}, s32[2,128]{1,0:T(2,128)}, u32[]{:S(2)}) copy-start(s32[2,128]{1,0:T(2,128)} %constant.218.clone.1) | copy-start | bytes 3076
  49.0 1.3 copy-start.2
  50.4 38.9 %all-to-all-start.1 = ((f32[128,32,128]{2,1,0:T(8,128)}), f32[128,32,128]{2,1,0:T(8,128)S(1)}, u32[]{:S(2)}, u32[]{:S(2)}) async-start(f32[128,32,128]{2,1,0:T(8,128)} %shard_map.77), calls=%async_computation.1 | async-start | bytes 4194304 | tf_op jit(solution)/shard_map/all_to_all | solution.py:383
  89.3 1.3 copy-start
  108.6 55.1 %all-to-all-start.2 = ((f32[128,32,128]{2,1,0:T(8,128)}), f32[128,32,128]{2,1,0:T(8,128)S(1)}, u32[]{:S(2)}, u32[]{:S(2)}) async-start(f32[128,32,128]{2,1,0:T(8,128)} %bitcast.77), calls=%async_computation.2 | async-start | bytes 4194304 | tf_op jit(solution)/shard_map/all_to_all | solution.py:391
  125.2 14.6 %collective-permute-start = (f32[4,40,128]{2,1,0:T(8,128)S(1)}, f32[4,40,128]{2,1,0:T(8,128)S(1)}, u32[]{:S(2)}, u32[]{:S(2)}) collective-permute-start(f32[4,40,128]{2,1,0:T(8,128)S(1)} %get-tuple-element.92), channel_id=1, source_target_pairs={{0,16},{8,24},{16,0},{24,8},{32,48},{40,56},{48,32},{56,40},{64,80... | collective-permute-start | bytes 245768 | tf_op jit(solution)/shard_map/ppermute | solution.py:419
  126.3 14.4 %collective-permute-start.1 = (f32[4,40,128]{2,1,0:T(8,128)S(1)}, f32[4,40,128]{2,1,0:T(8,128)S(1)}, u32[]{:S(2)}, u32[]{:S(2)}) collective-permute-start(f32[4,40,128]{2,1,0:T(8,128)S(1)} %get-tuple-element.91), channel_id=1, source_target_pairs={{0,8},{8,16},{16,24},{24,0},{32,40},{40,48},{48,56},{56,32},{64,72... | collective-permute-start | bytes 245768 | tf_op jit(solution)/shard_map/ppermute | solution.py:419
  126.3 14.4 %collective-permute-start.2 = (f32[4,40,128]{2,1,0:T(8,128)S(1)}, f32[4,40,128]{2,1,0:T(8,128)S(1)}, u32[]{:S(2)}, u32[]{:S(2)}) collective-permute-start(f32[4,40,128]{2,1,0:T(8,128)S(1)} %get-tuple-element.90), channel_id=1, source_target_pairs={{0,24},{8,0},{16,8},{24,16},{32,56},{40,32},{48,40},{56,48},{64,88... | collective-permute-start | bytes 245768 | tf_op jit(solution)/shard_map/ppermute | solution.py:419
  141.6 6.3 %collective-permute-start.3 = (f32[40,128]{1,0:T(8,128)S(1)}, f32[40,128]{1,0:T(8,128)S(1)}, u32[]{:S(2)}, u32[]{:S(2)}) collective-permute-start(f32[40,128]{1,0:T(8,128)S(1)} %get-tuple-element.107), channel_id=1, source_target_pairs={{0,64},{8,72},{16,80},{24,88},{32,96},{40,104},{48,112},{56,120},{... | collective-permute-start | bytes 61448 | tf_op jit(solution)/shard_map/ppermute | solution.py:419
  144.7 5.0 %collective-permute-start.4 = (f32[40,128]{1,0:T(8,128)S(1)}, f32[40,128]{1,0:T(8,128)S(1)}, u32[]{:S(2)}, u32[]{:S(2)}) collective-permute-start(f32[40,128]{1,0:T(8,128)S(1)} %get-tuple-element.106), channel_id=1, source_target_pairs={{0,32},{8,40},{16,48},{24,56},{32,64},{40,72},{48,80},{56,88},{64,... | collective-permute-start | bytes 61448 | tf_op jit(solution)/shard_map/ppermute | solution.py:419
  145.4 4.2 %collective-permute-start.5 = (f32[40,128]{1,0:T(8,128)S(1)}, f32[40,128]{1,0:T(8,128)S(1)}, u32[]{:S(2)}, u32[]{:S(2)}) collective-permute-start(f32[40,128]{1,0:T(8,128)S(1)} %get-tuple-element.105), channel_id=1, source_target_pairs={{0,96},{8,104},{16,112},{24,120},{32,0},{40,8},{48,16},{56,24},{64... | collective-permute-start | bytes 61448 | tf_op jit(solution)/shard_map/ppermute | solution.py:419
  149.7 6.9 %collective-permute-start.6 = (f32[40,128]{1,0:T(8,128)S(1)}, f32[40,128]{1,0:T(8,128)S(1)}, u32[]{:S(2)}, u32[]{:S(2)}) collective-permute-start(f32[40,128]{1,0:T(8,128)S(1)} %fusion.24), channel_id=1, source_target_pairs={{0,4},{1,5},{2,6},{3,7},{4,0},{5,1},{6,2},{7,3},{8,12},{9,13},{10,... | collective-permute-start | bytes 61448 | tf_op jit(solution)/shard_map/ppermute | solution.py:419
  153.3 5.0 %collective-permute-start.7 = (f32[40,128]{1,0:T(8,128)S(1)}, f32[40,128]{1,0:T(8,128)S(1)}, u32[]{:S(2)}, u32[]{:S(2)}) collective-permute-start(f32[40,128]{1,0:T(8,128)S(1)} %fusion.24), channel_id=1, source_target_pairs={{0,2},{1,3},{2,4},{3,5},{4,6},{5,7},{6,0},{7,1},{8,10},{9,11},{10,... | collective-permute-start | bytes 61448 | tf_op jit(solution)/shard_map/ppermute | solution.py:419
  154.1 4.2 %collective-permute-start.8 = (f32[40,128]{1,0:T(8,128)S(1)}, f32[40,128]{1,0:T(8,128)S(1)}, u32[]{:S(2)}, u32[]{:S(2)}) collective-permute-start(f32[40,128]{1,0:T(8,128)S(1)} %fusion.24), channel_id=1, source_target_pairs={{0,6},{1,7},{2,0},{3,1},{4,2},{5,3},{6,4},{7,5},{8,14},{9,15},{10,... | collective-permute-start | bytes 61448 | tf_op jit(solution)/shard_map/ppermute | solution.py:419
  158.3 5.4 %collective-permute-start.9 = (f32[40,128]{1,0:T(8,128)S(1)}, f32[40,128]{1,0:T(8,128)S(1)}, u32[]{:S(2)}, u32[]{:S(2)}) collective-permute-start(f32[40,128]{1,0:T(8,128)S(1)} %add_add_fusion), channel_id=1, source_target_pairs={{0,1},{1,0},{2,3},{3,2},{4,5},{5,4},{6,7},{7,6},{8,9},{9,8},{10,11... | collective-permute-start | bytes 61448 | tf_op jit(solution)/shard_map/ppermute | solution.py:419
  163.7 6.1 %copy-start.1 = (f32[128,32,128]{2,1,0:T(8,128)}, f32[128,32,128]{2,1,0:T(8,128)S(1)}, u32[]{:S(2)}) copy-start(f32[128,32,128]{2,1,0:T(8,128)S(1)} %all-to-all-done.2.blocks_ref) | copy-start | bytes 6291460
  164.4 10.8 %all-to-all-start.3 = ((f32[16,4,128]{2,1,0:T(4,128)}), f32[16,4,128]{2,1,0:T(4,128)S(1)}, u32[]{:S(2)}, u32[]{:S(2)}) async-start(f32[16,4,128]{2,1,0:T(4,128)} %broadcast_in_dim.26), calls=%async_computation.3 | async-start | bytes 65536 | tf_op jit(solution)/shard_map/all_to_all | solution.py:405
